TPU v7x, 32 devices: a whole 2x2x4 slice. The times are simulated.
32 devices in a mesh: seg: 8 (over z, core), bond: 4 (over y, x).
Axes of the slice: x: 2, y: 2, z: 4, core: 2. Of those that a mesh axis runs over, the one named last changes fastest.
Arguments:
- left_env: bfloat16 [8, 1024, 6, 1024], P('seg', 'bond'), may hold values from -0.1875 to 0.1875
- prev_left: bfloat16 [8, 1024, 1024], P('seg'), may hold values from -0.25 to 1.25
- cur_site: bfloat16 [8, 1024, 4, 1024], P('seg', 'bond'), may hold values from -6 to 6
- prev_site: bfloat16 [8, 1024, 4, 1024], P('seg', None, None, 'bond'), may hold values from -6 to 6
- hamiltonian: bfloat16 [8, 6, 6, 4, 4], P('seg'), may hold values from -1.25 to 1.25
- right_env: bfloat16 [8, 1024, 6, 1024], P('seg', 'bond'), may hold values from -0.078125 to 0.078125
- prev_right: bfloat16 [8, 1024, 1024], P('seg'), may hold values from -0.25 to 1.25
Outputs:
- new_site: bfloat16 [8, 1024, 4, 1024], P('seg', 'bond')
- center: float32 [8, 1024, 1024], P('seg', 'bond')
All inputs are finite; a program needn't handle non-finite values.
Results may differ from a plain program's by a relative error of at most 0.0054.
Values may be sent and summed in bfloat16 or wider, within the bound.
A program may use at most 128 MiB of HBM per device.

v0:
```python
import math
import jax
import jax.numpy as jnp
from jax import lax
from jax.sharding import PartitionSpec as P

PHYS = 4
MPOB = 6


def shifted(block, axis, distance):
    devices = range(lax.axis_size(axis))
    route = [((i - distance) % len(devices), i) for i in devices]
    return lax.ppermute(block, axis, route)


def shards(left_env, prev_left, cur_site, prev_site, hamiltonian, right_env, prev_right):
    left_now, prev_now = shifted((left_env[0], prev_left[0]), "seg", 1)
    own_rows = left_now.shape[0]
    bond_width = left_now.shape[2]
    coupling = hamiltonian[0].astype(jnp.float32)
    current = lax.all_gather(cur_site[0], "bond", axis=0, tiled=True)
    projected = jnp.dot(
        left_now.reshape(own_rows * MPOB, bond_width),
        current.reshape(bond_width, PHYS * bond_width),
        preferred_element_type=jnp.float32,
    ).reshape(own_rows, MPOB, PHYS, bond_width)
    mixture = jnp.einsum(
        "autc,uvst->asvc", projected, coupling, precision=lax.Precision.HIGHEST
    ).astype(jnp.bfloat16)
    applied = jnp.einsum(
        "asvc,cvy->asy",
        mixture,
        lax.all_gather(right_env[0], "bond", axis=0, tiled=True),
        preferred_element_type=jnp.float32,
    )
    partial_value = jnp.einsum(
        "ab,bsc->asc", prev_now, prev_site[0], preferred_element_type=jnp.float32
    ).astype(jnp.bfloat16)
    second = jnp.einsum(
        "akc,cy->aky",
        lax.all_to_all(partial_value, "bond", split_axis=0, concat_axis=2, tiled=True),
        prev_right[0],
        preferred_element_type=jnp.float32,
    )
    target = (2.0 * applied - second).reshape(own_rows * PHYS, bond_width)
    local_correlation = jnp.dot(
        target.T, target, precision=lax.Precision.HIGHEST, preferred_element_type=jnp.float32
    )
    correlation = lax.psum(local_correlation, "bond")
    triangle = jnp.linalg.cholesky(correlation)
    solved = jax.scipy.linalg.solve_triangular(triangle, target.T, lower=True)
    norming = math.sqrt(bond_width * PHYS)
    new_site = (solved.T * norming).astype(jnp.bfloat16).reshape(1, own_rows, PHYS, bond_width)
    offset = lax.axis_index("bond") * own_rows
    center = lax.dynamic_slice_in_dim(triangle.T, offset, own_rows, 0) / norming
    return (new_site, center[None])


def solution(mesh):
    return jax.shard_map(
        shards,
        mesh=mesh,
        in_specs=(
            P("seg", "bond", None, None),
            P("seg", None, None),
            P("seg", "bond", None, None),
            P("seg", None, None, "bond"),
            P("seg", None, None, None, None),
            P("seg", "bond", None, None),
            P("seg", None, None),
        ),
        out_specs=(P("seg", "bond", None, None), P("seg", "bond", None)),
        check_vma=False,
    )
```

profile of v0, /device:TPU:0, one launch (start us, length us, event | category | flops | bytes accessed | tf_op | source)
XLA Modules:
  0.0 759.1 jit_solution(3926485406650583413)
XLA Ops:
  9.3 2.7 collective-permute-start
  11.9 25.3 %collective-permute-done.1 = bf16[1024,1024]{1,0:T(8,128)(2,1)S(1)} collective-permute-done((bf16[1024,1024]{1,0:T(8,128)(2,1)}, bf16[1024,1024]{1,0:T(8,128)(2,1)S(1)}, u32[]{:S(2)}, u32[]{:S(2)}) %collective-permute-start.1) | collective-permute-done | bytes 2097184 | tf_op jit(solution)/shard_map/ppermute | solution.py:14
  37.2 2.3 fusion.31
  41.2 40.1 %all_to_all.18 = bf16[1024,4,256]{2,1,0:T(4,128)(2,1)S(1)} all-to-all(bf16[1024,4,256]{2,1,0:T(4,128)(2,1)S(1)} %copy.30), channel_id=1, replica_groups=mesh['seg'=8,'bond'=4] {'bond'}, dimensions={0} | all-to-all | bytes 4194304 | tf_op jit(solution)/shard_map/all_to_all | solution.py:42
  82.9 2.7 all_to_all.16
  85.6 6.5 fusion.26
  92.1 22.9 %all-gather.5.cloned.1.call-done = bf16[1,1024,4,1024]{3,2,0,1:T(4,128)(2,1)} async-done(((bf16[1,256,4,1024]{3,2,0,1:T(4,128)(2,1)}), bf16[1,1024,4,1024]{3,2,0,1:T(4,128)(2,1)}) %all-gather.5.cloned.1.call-update) | async-done | bytes 8388624 | tf_op jit(solution)/shard_map/all_gather | solution.py:22
  115.0 14.1 %copy.45 = bf16[1,1024,4,1024]{1,3,2,0:T(8,128)(2,1)} copy(bf16[1,1024,4,1024]{3,2,0,1:T(4,128)(2,1)} %all-gather.5.cloned.1.call-done) | data formatting | bytes 16777216 | tf_op jit(solution)/shard_map/reshape | solution.py:25
  129.1 21.9 %convolution_bitcast_fusion = f32[256,6,4,1024,1]{3,0,2,1,4:T(8,128)} fusion(bf16[1,1024,4,1024]{1,3,2,0:T(8,128)(2,1)} %copy.45, bf16[256,6,1024]{2,0,1:T(8,128)(2,1)} %collective-permute-done), kind=kOutput, calls=%fused_computation.9 | convolution fusion | flops 12884901888 | bytes 36700160 | tf_op jit(solution)/shard_map/dot_general | solution.py:23
  151.0 62.8 %fusion.2 = bf16[256,4,6,1024]{3,2,1,0:T(8,128)(2,1)} fusion(f32[256,6,4,1024,1]{3,0,2,1,4:T(8,128)} %convolution_bitcast_fusion, bf16[1,6,6,4,4]{2,4,3,1,0:T(4,128)(2,1)S(1)} %copy-done.5), kind=kOutput, calls=%fused_computation.5 | convolution fusion | flops 1818230784 | bytes 37749888 | tf_op jit(solution)/shard_map/autc,uvst->asvc/dot_general | solution.py:28
  213.7 25.5 %all-gather.7.cloned.1.call-done = bf16[1,1024,6,1024]{3,1,2,0:T(8,128)(2,1)} async-done(((bf16[1,256,6,1024]{3,1,2,0:T(8,128)(2,1)}), bf16[1,1024,6,1024]{3,1,2,0:T(8,128)(2,1)}) %all-gather.7.cloned.1.call-update) | async-done | bytes 12582928 | tf_op jit(solution)/shard_map/all_gather | solution.py:34
  239.2 32.4 %fusion.10 = f32[256,4,1024]{2,0,1:T(8,128)S(1)} fusion(f32[256,4,1024]{2,0,1:T(8,128)} %fusion.26, bf16[1,1024,6,1024]{3,1,2,0:T(8,128)(2,1)} %all-gather.7.cloned.1.call-done, bf16[256,4,6,1024]{3,2,1,0:T(8,128)(2,1)} %fusion.2), kind=kOutput, calls=%fused_computation.14 | convolution fusion | flops 12886999040 | bytes 33554432 | tf_op jit(solution)/shard_map/asvc,cvy->asy/dot_general | solution.py:31
  271.7 1.9 copy-done.4
  273.6 15.1 %convolution_bitcast_fusion.1 = f32[1024,1024]{0,1:T(8,128)} fusion(f32[256,4,1024]{2,0,1:T(8,128)S(1)} %fusion.10), kind=kOutput, calls=%fused_computation.20 | convolution fusion | flops 12884901888 | bytes 8388608 | tf_op jit(solution)/shard_map/dot_general | solution.py:47
  288.8 6.8 copy.35
  295.6 5.3 reshape.94
  300.9 5.5 copy.36
  306.4 86.1 %all-reduce.3.cloned.1.call-done = f32[1024,1024]{0,1:T(8,128)} async-done(((f32[1024,1024]{0,1:T(8,128)}), f32[1024,1024]{0,1:T(8,128)}) %all-reduce.3.cloned.1.call-update) | async-done | bytes 4194320 | tf_op jit(solution)/shard_map/psum | solution.py:50
  392.5 5.7 copy.34
  398.3 4.4 fusion.9
  402.7 2.0 copy-done.3
  404.7 11.7 %cholesky.223 = f32[128,128]{1,0:T(8,128)S(1)} custom-call(f32[128,128]{1,0:T(8,128)S(1)} %cholesky.580), custom_call_target="Cholesky" | custom-call | tf_op jit(solution)/shard_map/jit(cholesky)/cholesky | solution.py:51
  416.4 9.8 %custom-call.63 = f32[1,128,128]{1,2,0:T(8,128)S(1)} custom-call(f32[1,128,128]{2,1,0:T(8,128)S(1)} %get-tuple-element.74), custom_call_target="InvertDiagBlocksLowerTriangular" | custom-call | tf_op jit(solution)/shard_map/jit(cholesky)/cholesky | solution.py:51
  426.3 2.5 cholesky.255
  428.7 2.4 constant_dynamic-update-slice_fusion.32
  432.7 11.9 %cholesky.244 = f32[128,128]{1,0:T(8,128)S(1)} custom-call(f32[128,128]{1,0:T(8,128)S(1)} %cholesky.584), custom_call_target="Cholesky" | custom-call | tf_op jit(solution)/shard_map/jit(cholesky)/cholesky | solution.py:51
  445.2 9.8 %custom-call.64 = f32[1,128,128]{1,2,0:T(8,128)S(1)} custom-call(f32[1,128,128]{2,1,0:T(8,128)S(1)} %get-tuple-element.71), custom_call_target="InvertDiagBlocksLowerTriangular" | custom-call | tf_op jit(solution)/shard_map/jit(cholesky)/cholesky | solution.py:51
  456.3 2.1 convolution_subtract_fusion.6
  458.4 11.7 %cholesky.468 = f32[128,128]{1,0:T(8,128)S(1)} custom-call(f32[128,128]{1,0:T(8,128)S(1)} %cholesky.589), custom_call_target="Cholesky" | custom-call | tf_op jit(solution)/shard_map/jit(cholesky)/cholesky | solution.py:51
  471.4 9.8 %custom-call.65 = f32[1,128,128]{1,2,0:T(8,128)S(1)} custom-call(f32[1,128,128]{2,1,0:T(8,128)S(1)} %get-tuple-element.68), custom_call_target="InvertDiagBlocksLowerTriangular" | custom-call | tf_op jit(solution)/shard_map/jit(cholesky)/cholesky | solution.py:51
  482.4 2.3 convolution_subtract_fusion.7
  484.7 11.9 %cholesky.487 = f32[128,128]{1,0:T(8,128)S(1)} custom-call(f32[128,128]{1,0:T(8,128)S(1)} %cholesky.594), custom_call_target="Cholesky" | custom-call | tf_op jit(solution)/shard_map/jit(cholesky)/cholesky | solution.py:51
  497.9 9.8 %custom-call.66 = f32[1,128,128]{1,2,0:T(8,128)S(1)} custom-call(f32[1,128,128]{2,1,0:T(8,128)S(1)} %get-tuple-element.65), custom_call_target="InvertDiagBlocksLowerTriangular" | custom-call | tf_op jit(solution)/shard_map/jit(cholesky)/cholesky | solution.py:51
  508.8 2.3 convolution_subtract_fusion.8
  511.2 11.7 %cholesky.506 = f32[128,128]{1,0:T(8,128)S(1)} custom-call(f32[128,128]{1,0:T(8,128)S(1)} %cholesky.599), custom_call_target="Cholesky" | custom-call | tf_op jit(solution)/shard_map/jit(cholesky)/cholesky | solution.py:51
  524.2 10.2 %custom-call.67 = f32[1,128,128]{1,2,0:T(8,128)S(1)} custom-call(f32[1,128,128]{2,1,0:T(8,128)S(1)} %get-tuple-element.62), custom_call_target="InvertDiagBlocksLowerTriangular" | custom-call | tf_op jit(solution)/shard_map/jit(cholesky)/cholesky | solution.py:51
  535.4 2.3 convolution_subtract_fusion.9
  537.7 11.7 %cholesky.526 = f32[128,128]{1,0:T(8,128)S(1)} custom-call(f32[128,128]{1,0:T(8,128)S(1)} %cholesky.604), custom_call_target="Cholesky" | custom-call | tf_op jit(solution)/shard_map/jit(cholesky)/cholesky | solution.py:51
  550.7 9.8 %custom-call.68 = f32[1,128,128]{1,2,0:T(8,128)S(1)} custom-call(f32[1,128,128]{2,1,0:T(8,128)S(1)} %get-tuple-element.59), custom_call_target="InvertDiagBlocksLowerTriangular" | custom-call | tf_op jit(solution)/shard_map/jit(cholesky)/cholesky | solution.py:51
  561.4 2.0 convolution_subtract_fusion.10
  563.5 11.9 %cholesky.546 = f32[128,128]{1,0:T(8,128)S(1)} custom-call(f32[128,128]{1,0:T(8,128)S(1)} %cholesky.609), custom_call_target="Cholesky" | custom-call | tf_op jit(solution)/shard_map/jit(cholesky)/cholesky | solution.py:51
  576.6 9.8 %custom-call.69 = f32[1,128,128]{1,2,0:T(8,128)S(1)} custom-call(f32[1,128,128]{2,1,0:T(8,128)S(1)} %get-tuple-element.56), custom_call_target="InvertDiagBlocksLowerTriangular" | custom-call | tf_op jit(solution)/shard_map/jit(cholesky)/cholesky | solution.py:51
  587.2 1.8 convolution_subtract_fusion.11
  589.0 11.7 %cholesky.564 = f32[128,128]{1,0:T(8,128)S(1)} custom-call(f32[128,128]{1,0:T(8,128)S(1)} %convolution_subtract_fusion.11), custom_call_target="Cholesky" | custom-call | tf_op jit(solution)/shard_map/jit(cholesky)/cholesky | solution.py:51
  607.6 6.7 fusion.11
  614.3 23.0 %while.1 = (s32[]{:T(128)}, f32[1024,1024]{1,0:T(8,128)}, s32[8,2]{0,1:T(2,128)S(1)}, f32[8,128,128]{2,1,0:T(8,128)S(1)}, s32[]{:T(128)}) while((s32[]{:T(128)}, f32[1024,1024]{1,0:T(8,128)}, s32[8,2]{0,1:T(2,128)S(1)}, f32[8,128,128]{2,1,0:T(8,128)S(1)}, s32[]{:T(128)}) %tuple.65), condition=%wide.while_cond, body=%wide.while_body.sunk | while | flops 2 | bytes 131181 | solution.py:52
  614.9 2.3 bitcast_dynamic-update-slice_fusion.2
  617.8 2.3 bitcast_dynamic-update-slice_fusion.2
  620.7 2.3 bitcast_dynamic-update-slice_fusion.2
  623.6 2.3 bitcast_dynamic-update-slice_fusion.2
  626.5 2.3 bitcast_dynamic-update-slice_fusion.2
  629.4 2.3 bitcast_dynamic-update-slice_fusion.2
  632.3 2.3 bitcast_dynamic-update-slice_fusion.2
  635.1 2.2 bitcast_dynamic-update-slice_fusion.2
  637.3 78.8 %custom-call.70 = f32[8,128,128]{1,2,0:T(8,128)S(1)} custom-call(f32[8,128,128]{2,1,0:T(8,128)S(1)} %get-tuple-element.9), custom_call_target="InvertDiagBlocksLowerTriangular" | custom-call | tf_op jit(solution)/shard_map/jit(_solve_triangular)/triangular_solve | solution.py:52
  716.2 1.9 constant_dynamic-update-slice_fusion.17
  722.9 2.0 fusion.42
  725.7 2.2 fusion.45
  728.6 2.6 convolution_subtract_fusion.2
  732.0 2.8 convolution_subtract_fusion.1
  735.4 3.5 convolution_subtract_fusion.3
  739.6 1.9 fusion.17
  741.5 4.1 copy.37
  745.6 4.1 reshape.95
  (79 shorter events, 38.0 us)
Async XLA Ops:
  7.2 30.0 %copy-start = (bf16[1,1024,4,256]{3,2,1,0:T(4,128)(2,1)S(1)}, bf16[1,1024,4,256]{3,2,1,0:T(4,128)(2,1)}, u32[]{:S(2)}) copy-start(bf16[1,1024,4,256]{3,2,1,0:T(4,128)(2,1)} %param.10) | copy-start | bytes 6291460
  7.2 107.8 %all-gather.5.cloned.1.call-start = ((), (), s32[]{:S(2)}) async-start(), calls=%async_computation.2 | async-start | bytes 10485760 | tf_op jit(solution)/shard_map/all_gather | solution.py:22
  7.9 231.3 %all-gather.7.cloned.1.call-start = ((), (), s32[]{:S(2)}) async-start(), calls=%async_computation.3 | async-start | bytes 15728640 | tf_op jit(solution)/shard_map/all_gather | solution.py:34
  8.7 383.9 %all-reduce.3.cloned.1.call-start = ((), (), s32[]{:S(2)}) async-start(), calls=%async_computation.1 | async-start | bytes 8388608 | tf_op jit(solution)/shard_map/psum | solution.py:50
  8.7 28.5 %collective-permute-start.1 = (bf16[1024,1024]{1,0:T(8,128)(2,1)}, bf16[1024,1024]{1,0:T(8,128)(2,1)S(1)}, u32[]{:S(2)}, u32[]{:S(2)}) collective-permute-start(bf16[1024,1024]{1,0:T(8,128)(2,1)} %bitcast.186), channel_id=1, source_target_pairs={{28,0},{0,4},{4,8},{8,12},{12,16},{16,20},{20,24},{24,28},{29,1},{... | collective-permute-start | bytes 6291464 | tf_op jit(solution)/shard_map/ppermute | solution.py:14
  9.3 119.9 %collective-permute-start = (bf16[256,6,1024]{2,0,1:T(8,128)(2,1)}, bf16[256,6,1024]{2,0,1:T(8,128)(2,1)}, u32[]{:S(2)}, u32[]{:S(2)}) collective-permute-start(bf16[256,6,1024]{2,0,1:T(8,128)(2,1)} %bitcast.185), channel_id=1, source_target_pairs={{28,0},{0,4},{4,8},{8,12},{12,16},{16,20},{20,24},{24,28},{29,1},{... | collective-permute-start | bytes 9437192 | tf_op jit(solution)/shard_map/ppermute | solution.py:14
  129.1 21.9 %copy-start.5 = (bf16[1,6,6,4,4]{2,4,3,1,0:T(4,128)(2,1)S(1)}, bf16[1,6,6,4,4]{2,4,3,1,0:T(4,128)(2,1)}, u32[]{:S(2)}) copy-start(bf16[1,6,6,4,4]{2,4,3,1,0:T(4,128)(2,1)} %param.11) | copy-start | bytes 3460
  271.7 1.9 copy-start.4
  402.7 2.0 copy-start.3
  716.2 4.3 copy-start.2
  741.5 10.8 %copy-start.1 = (bf16[1,1024,4,256]{3,2,1,0:T(4,128)(2,1)S(1)}, bf16[1,1024,4,256]{3,2,1,0:T(4,128)(2,1)}, u32[]{:S(2)}) copy-start(bf16[1,1024,4,256]{3,2,1,0:T(4,128)(2,1)} %param.10) | copy-start | bytes 6291460
Sparse Core Ops, SparseCore 0:
  9.8 105.0 all-gather.4
  116.8 122.3 all-gather.6
  288.9 103.5 all-reduce.2
where the time goes:
time: 764 us; the launch traced here: 759 us
  other arithmetic  265 us (35%)
  matrix products  187 us (24%)
  waiting for transfers between devices  161 us (21%)
  local copies, waits for them, and re-layouts  82.3 us (11%)
  blocking collectives  40.1 us (5%)
  between operations  19.3 us (3%)
    another operation x30, other arithmetic, shards(): triangle = jnp.linalg.cholesky(correlation)  172 us
    psum x1, waiting for transfers between devices, shards(): correlation = lax.psum(local_correlation, 'bond')  86.1 us
    another operation x3, other arithmetic, shards(): solved = jax.scipy.linalg.solve_triangular(triangle, target.T, lower=True)  85.5 us
    dot_general x1, matrix products, shards(): jnp.einsum('autc,uvst->asvc', projected, coupling, precision=lax.Precisio...  62.8 us
    all_to_all x1, blocking collectives, shards(): lax.all_to_all(partial_value, 'bond', split_axis=0, concat_axis=2, tiled=...  40.1 us
    dot_general x1, matrix products, shards(): jnp.einsum('asvc,cvy->asy', mixture, lax.all_gather(right_env[0], 'bond',...  32.4 us
    all_gather x1, waiting for transfers between devices, shards(): lax.all_gather(right_env[0], 'bond', axis=0, tiled=True)  25.5 us
    ppermute x2, waiting for transfers between devices, shifted(): return lax.ppermute(block, axis, route)  25.3 us
  transfers between devices with their start and end apart: 5, of which 4 were waited for; matrix products, arithmetic and copies ran while one was open for 17% of the time, Pallas kernels for 0%

commit v1 on v0

--- a/solution.py
+++ b/solution.py
@@ -47,7 +47,7 @@
     local_correlation = jnp.dot(
         target.T, target, precision=lax.Precision.HIGHEST, preferred_element_type=jnp.float32
     )
-    correlation = lax.psum(local_correlation, "bond")
+    correlation = jnp.sum(lax.all_gather(local_correlation, "bond"), axis=0)
     triangle = jnp.linalg.cholesky(correlation)
     solved = jax.scipy.linalg.solve_triangular(triangle, target.T, lower=True)
     norming = math.sqrt(bond_width * PHYS)

time: 764 us -> 828 us (1.084)
  waiting for transfers between devices: 161 us -> 214 us
  other arithmetic: 265 us -> 276 us
    all_gather x0 -> x1, waiting for transfers between devices: none -> 139 us  [shards(): correlation = jnp.sum(lax.all_gather(local_correlation, 'bond'), axis=0)]
    psum x1 -> x0, waiting for transfers between devices: 86.1 us -> none  [shards(): correlation = lax.psum(local_correlation, 'bond')]
    reduce_sum x0 -> x1, other arithmetic: none -> 10.3 us  [shards(): correlation = jnp.sum(lax.all_gather(local_correlation, 'bond'), axis=0)]
  transfers between devices with their start and end apart: 5 -> 5, of which waited for: 4 -> 4; matrix products, arithmetic and copies ran while one was open for 17% -> 16% of each run, Pallas kernels for 0% -> 0%
where the time goes in v1:
time: 828 us; the launch traced here: 823 us
  other arithmetic  276 us (33%)
  waiting for transfers between devices  214 us (26%)
  matrix products  187 us (23%)
  local copies, waits for them, and re-layouts  82.5 us (10%)
  blocking collectives  40.1 us (5%)
  between operations  19.4 us (2%)
    another operation x30, other arithmetic, shards(): triangle = jnp.linalg.cholesky(correlation)  172 us
    all_gather x1, waiting for transfers between devices, shards(): correlation = jnp.sum(lax.all_gather(local_correlation, 'bond'), axis=0)  139 us
    another operation x3, other arithmetic, shards(): solved = jax.scipy.linalg.solve_triangular(triangle, target.T, lower=True)  85.4 us
    dot_general x1, matrix products, shards(): jnp.einsum('autc,uvst->asvc', projected, coupling, precision=lax.Precisio...  62.9 us
    all_to_all x1, blocking collectives, shards(): lax.all_to_all(partial_value, 'bond', split_axis=0, concat_axis=2, tiled=...  40.1 us
    dot_general x1, matrix products, shards(): jnp.einsum('asvc,cvy->asy', mixture, lax.all_gather(right_env[0], 'bond',...  32.4 us
    all_gather x1, waiting for transfers between devices, shards(): lax.all_gather(right_env[0], 'bond', axis=0, tiled=True)  25.4 us
    ppermute x2, waiting for transfers between devices, shifted(): return lax.ppermute(block, axis, route)  25.3 us
  transfers between devices with their start and end apart: 5, of which 4 were waited for; matrix products, arithmetic and copies ran while one was open for 16% of the time, Pallas kernels for 0%

profile of v1, /device:TPU:0, one launch (start us, length us, event | category | flops | bytes accessed | tf_op | source)
XLA Modules:
  0.0 822.7 jit_solution(15423488302968876077)
XLA Ops:
  9.3 2.7 collective-permute-start
  11.9 25.3 %collective-permute-done.1 = bf16[1024,1024]{1,0:T(8,128)(2,1)S(1)} collective-permute-done((bf16[1024,1024]{1,0:T(8,128)(2,1)}, bf16[1024,1024]{1,0:T(8,128)(2,1)S(1)}, u32[]{:S(2)}, u32[]{:S(2)}) %collective-permute-start.1) | collective-permute-done | bytes 2097184 | tf_op jit(solution)/shard_map/ppermute | solution.py:14
  37.2 2.3 fusion.31
  41.2 40.1 %all_to_all.18 = bf16[1024,4,256]{2,1,0:T(4,128)(2,1)S(1)} all-to-all(bf16[1024,4,256]{2,1,0:T(4,128)(2,1)S(1)} %copy.28), channel_id=1, replica_groups=mesh['seg'=8,'bond'=4] {'bond'}, dimensions={0} | all-to-all | bytes 4194304 | tf_op jit(solution)/shard_map/all_to_all | solution.py:42
  82.9 2.7 all_to_all.16
  85.6 6.5 fusion.26
  92.1 22.9 %all-gather.7.cloned.1.call-done = bf16[1,1024,4,1024]{3,2,0,1:T(4,128)(2,1)} async-done(((bf16[1,256,4,1024]{3,2,0,1:T(4,128)(2,1)}), bf16[1,1024,4,1024]{3,2,0,1:T(4,128)(2,1)}) %all-gather.7.cloned.1.call-update) | async-done | bytes 8388624 | tf_op jit(solution)/shard_map/all_gather | solution.py:22
  115.0 14.1 %copy.41 = bf16[1,1024,4,1024]{1,3,2,0:T(8,128)(2,1)} copy(bf16[1,1024,4,1024]{3,2,0,1:T(4,128)(2,1)} %all-gather.7.cloned.1.call-done) | data formatting | bytes 16777216 | tf_op jit(solution)/shard_map/reshape | solution.py:25
  129.1 21.9 %convolution_bitcast_fusion = f32[256,6,4,1024,1]{3,0,2,1,4:T(8,128)} fusion(bf16[1,1024,4,1024]{1,3,2,0:T(8,128)(2,1)} %copy.41, bf16[256,6,1024]{2,0,1:T(8,128)(2,1)} %collective-permute-done), kind=kOutput, calls=%fused_computation.9 | convolution fusion | flops 12884901888 | bytes 36700160 | tf_op jit(solution)/shard_map/dot_general | solution.py:23
  151.0 62.9 %fusion.2 = bf16[256,4,6,1024]{3,2,1,0:T(8,128)(2,1)} fusion(f32[256,6,4,1024,1]{3,0,2,1,4:T(8,128)} %convolution_bitcast_fusion, bf16[1,6,6,4,4]{2,4,3,1,0:T(4,128)(2,1)S(1)} %copy-done.5), kind=kOutput, calls=%fused_computation.5 | convolution fusion | flops 1818230784 | bytes 37749888 | tf_op jit(solution)/shard_map/autc,uvst->asvc/dot_general | solution.py:28
  213.8 25.4 %all-gather.9.cloned.1.call-done = bf16[1,1024,6,1024]{3,1,2,0:T(8,128)(2,1)} async-done(((bf16[1,256,6,1024]{3,1,2,0:T(8,128)(2,1)}), bf16[1,1024,6,1024]{3,1,2,0:T(8,128)(2,1)}) %all-gather.9.cloned.1.call-update) | async-done | bytes 12582928 | tf_op jit(solution)/shard_map/all_gather | solution.py:34
  239.2 32.4 %fusion.10 = f32[256,4,1024]{2,0,1:T(8,128)S(1)} fusion(f32[256,4,1024]{2,0,1:T(8,128)} %fusion.26, bf16[1,1024,6,1024]{3,1,2,0:T(8,128)(2,1)} %all-gather.9.cloned.1.call-done, bf16[256,4,6,1024]{3,2,1,0:T(8,128)(2,1)} %fusion.2), kind=kOutput, calls=%fused_computation.14 | convolution fusion | flops 12886999040 | bytes 33554432 | tf_op jit(solution)/shard_map/asvc,cvy->asy/dot_general | solution.py:31
  271.7 1.9 copy-done.4
  273.6 15.1 %convolution_bitcast_fusion.1 = f32[1024,1024]{1,0:T(8,128)} fusion(f32[256,4,1024]{2,0,1:T(8,128)S(1)} %fusion.10), kind=kOutput, calls=%fused_computation.20 | convolution fusion | flops 12884901888 | bytes 8388608 | tf_op jit(solution)/shard_map/dot_general | solution.py:47
  288.8 6.9 copy.32
  295.6 5.9 reshape.94
  301.6 5.6 copy.33
  307.1 139.0 %all-gather.11.cloned.1.call-done = f32[4096,1024]{1,0:T(8,128)} async-done(((f32[1024,1024]{1,0:T(8,128)}), f32[4096,1024]{1,0:T(8,128)}) %all-gather.11.cloned.1.call-update) | async-done | bytes 16777232 | tf_op jit(solution)/shard_map/all_gather | solution.py:50
  446.2 10.3 %reduce_sum.9 = f32[1024,1024]{1,0:T(8,128)} reduce(f32[4,1024,1024]{2,1,0:T(8,128)} %bitcast.175, f32[]{:T(128)} %constant.278.clone.1), dimensions={0}, to_apply=%region_0.0 | reduce | flops 3145728 | bytes 20971524 | tf_op jit(solution)/shard_map/reduce_sum | solution.py:50
  456.5 5.7 copy.31
  462.2 4.4 fusion.9
  466.7 1.9 copy-done.3
  468.6 11.7 %cholesky.223 = f32[128,128]{1,0:T(8,128)S(1)} custom-call(f32[128,128]{1,0:T(8,128)S(1)} %cholesky.580), custom_call_target="Cholesky" | custom-call | tf_op jit(solution)/shard_map/jit(cholesky)/cholesky | solution.py:51
  480.4 2.5 cholesky.255
  482.9 9.8 %custom-call.63 = f32[1,128,128]{1,2,0:T(8,128)S(1)} custom-call(f32[1,128,128]{2,1,0:T(8,128)S(1)} %get-tuple-element.74), custom_call_target="InvertDiagBlocksLowerTriangular" | custom-call | tf_op jit(solution)/shard_map/jit(cholesky)/cholesky | solution.py:51
  492.7 2.3 constant_dynamic-update-slice_fusion.32
  496.6 11.9 %cholesky.244 = f32[128,128]{1,0:T(8,128)S(1)} custom-call(f32[128,128]{1,0:T(8,128)S(1)} %cholesky.584), custom_call_target="Cholesky" | custom-call | tf_op jit(solution)/shard_map/jit(cholesky)/cholesky | solution.py:51
  509.1 9.8 %custom-call.64 = f32[1,128,128]{1,2,0:T(8,128)S(1)} custom-call(f32[1,128,128]{2,1,0:T(8,128)S(1)} %get-tuple-element.71), custom_call_target="InvertDiagBlocksLowerTriangular" | custom-call | tf_op jit(solution)/shard_map/jit(cholesky)/cholesky | solution.py:51
  520.2 2.1 convolution_subtract_fusion.6
  522.3 11.7 %cholesky.468 = f32[128,128]{1,0:T(8,128)S(1)} custom-call(f32[128,128]{1,0:T(8,128)S(1)} %cholesky.589), custom_call_target="Cholesky" | custom-call | tf_op jit(solution)/shard_map/jit(cholesky)/cholesky | solution.py:51
  535.3 9.8 %custom-call.65 = f32[1,128,128]{1,2,0:T(8,128)S(1)} custom-call(f32[1,128,128]{2,1,0:T(8,128)S(1)} %get-tuple-element.68), custom_call_target="InvertDiagBlocksLowerTriangular" | custom-call | tf_op jit(solution)/shard_map/jit(cholesky)/cholesky | solution.py:51
  546.3 2.3 convolution_subtract_fusion.7
  548.6 11.9 %cholesky.487 = f32[128,128]{1,0:T(8,128)S(1)} custom-call(f32[128,128]{1,0:T(8,128)S(1)} %cholesky.594), custom_call_target="Cholesky" | custom-call | tf_op jit(solution)/shard_map/jit(cholesky)/cholesky | solution.py:51
  561.8 9.8 %custom-call.66 = f32[1,128,128]{1,2,0:T(8,128)S(1)} custom-call(f32[1,128,128]{2,1,0:T(8,128)S(1)} %get-tuple-element.65), custom_call_target="InvertDiagBlocksLowerTriangular" | custom-call | tf_op jit(solution)/shard_map/jit(cholesky)/cholesky | solution.py:51
  572.7 2.3 convolution_subtract_fusion.8
  575.1 11.7 %cholesky.506 = f32[128,128]{1,0:T(8,128)S(1)} custom-call(f32[128,128]{1,0:T(8,128)S(1)} %cholesky.599), custom_call_target="Cholesky" | custom-call | tf_op jit(solution)/shard_map/jit(cholesky)/cholesky | solution.py:51
  588.2 10.2 %custom-call.67 = f32[1,128,128]{1,2,0:T(8,128)S(1)} custom-call(f32[1,128,128]{2,1,0:T(8,128)S(1)} %get-tuple-element.62), custom_call_target="InvertDiagBlocksLowerTriangular" | custom-call | tf_op jit(solution)/shard_map/jit(cholesky)/cholesky | solution.py:51
  599.4 2.3 convolution_subtract_fusion.9
  601.7 11.7 %cholesky.526 = f32[128,128]{1,0:T(8,128)S(1)} custom-call(f32[128,128]{1,0:T(8,128)S(1)} %cholesky.604), custom_call_target="Cholesky" | custom-call | tf_op jit(solution)/shard_map/jit(cholesky)/cholesky | solution.py:51
  614.7 9.8 %custom-call.68 = f32[1,128,128]{1,2,0:T(8,128)S(1)} custom-call(f32[1,128,128]{2,1,0:T(8,128)S(1)} %get-tuple-element.59), custom_call_target="InvertDiagBlocksLowerTriangular" | custom-call | tf_op jit(solution)/shard_map/jit(cholesky)/cholesky | solution.py:51
  625.4 2.0 convolution_subtract_fusion.10
  627.5 11.9 %cholesky.546 = f32[128,128]{1,0:T(8,128)S(1)} custom-call(f32[128,128]{1,0:T(8,128)S(1)} %cholesky.609), custom_call_target="Cholesky" | custom-call | tf_op jit(solution)/shard_map/jit(cholesky)/cholesky | solution.py:51
  640.6 9.8 %custom-call.69 = f32[1,128,128]{1,2,0:T(8,128)S(1)} custom-call(f32[1,128,128]{2,1,0:T(8,128)S(1)} %get-tuple-element.56), custom_call_target="InvertDiagBlocksLowerTriangular" | custom-call | tf_op jit(solution)/shard_map/jit(cholesky)/cholesky | solution.py:51
  653.0 11.7 %cholesky.564 = f32[128,128]{1,0:T(8,128)S(1)} custom-call(f32[128,128]{1,0:T(8,128)S(1)} %convolution_subtract_fusion.11), custom_call_target="Cholesky" | custom-call | tf_op jit(solution)/shard_map/jit(cholesky)/cholesky | solution.py:51
  671.7 6.6 fusion.11
  678.3 22.6 %while.1 = (s32[]{:T(128)}, f32[1024,1024]{1,0:T(8,128)}, s32[8,2]{0,1:T(2,128)S(1)}, f32[8,128,128]{2,1,0:T(8,128)S(1)}, s32[]{:T(128)}) while((s32[]{:T(128)}, f32[1024,1024]{1,0:T(8,128)}, s32[8,2]{0,1:T(2,128)S(1)}, f32[8,128,128]{2,1,0:T(8,128)S(1)}, s32[]{:T(128)}) %tuple.65), condition=%wide.while_cond, body=%wide.while_body.sunk | while | flops 2 | bytes 131181 | solution.py:52
  678.9 2.2 bitcast_dynamic-update-slice_fusion.2
  681.8 2.2 bitcast_dynamic-update-slice_fusion.2
  684.6 2.2 bitcast_dynamic-update-slice_fusion.2
  687.4 2.2 bitcast_dynamic-update-slice_fusion.2
  690.3 2.2 bitcast_dynamic-update-slice_fusion.2
  693.1 2.2 bitcast_dynamic-update-slice_fusion.2
  695.9 2.2 bitcast_dynamic-update-slice_fusion.2
  698.8 2.1 bitcast_dynamic-update-slice_fusion.2
  700.9 78.8 %custom-call.70 = f32[8,128,128]{1,2,0:T(8,128)S(1)} custom-call(f32[8,128,128]{2,1,0:T(8,128)S(1)} %get-tuple-element.9), custom_call_target="InvertDiagBlocksLowerTriangular" | custom-call | tf_op jit(solution)/shard_map/jit(_solve_triangular)/triangular_solve | solution.py:52
  779.8 1.9 constant_dynamic-update-slice_fusion.17
  786.5 2.0 fusion.42
  789.3 2.2 fusion.45
  792.2 2.6 convolution_subtract_fusion.2
  795.5 2.8 convolution_subtract_fusion.1
  799.0 3.5 convolution_subtract_fusion.3
  803.2 1.9 fusion.17
  805.1 4.1 copy.34
  809.2 4.1 reshape.95
  (80 shorter events, 39.7 us)
Async XLA Ops:
  7.2 30.0 %copy-start = (bf16[1,1024,4,256]{3,2,1,0:T(4,128)(2,1)S(1)}, bf16[1,1024,4,256]{3,2,1,0:T(4,128)(2,1)}, u32[]{:S(2)}) copy-start(bf16[1,1024,4,256]{3,2,1,0:T(4,128)(2,1)} %param.10) | copy-start | bytes 6291460
  7.2 107.8 %all-gather.7.cloned.1.call-start = ((), (), s32[]{:S(2)}) async-start(), calls=%async_computation.1 | async-start | bytes 10485760 | tf_op jit(solution)/shard_map/all_gather | solution.py:22
  7.9 231.3 %all-gather.9.cloned.1.call-start = ((), (), s32[]{:S(2)}) async-start(), calls=%async_computation.2 | async-start | bytes 15728640 | tf_op jit(solution)/shard_map/all_gather | solution.py:34
  8.7 437.5 %all-gather.11.cloned.1.call-start = ((), (), s32[]{:S(2)}) async-start(), calls=%async_computation.3 | async-start | bytes 20971520 | tf_op jit(solution)/shard_map/all_gather | solution.py:50
  8.7 28.5 %collective-permute-start.1 = (bf16[1024,1024]{1,0:T(8,128)(2,1)}, bf16[1024,1024]{1,0:T(8,128)(2,1)S(1)}, u32[]{:S(2)}, u32[]{:S(2)}) collective-permute-start(bf16[1024,1024]{1,0:T(8,128)(2,1)} %bitcast.188), channel_id=1, source_target_pairs={{28,0},{0,4},{4,8},{8,12},{12,16},{16,20},{20,24},{24,28},{29,1},{... | collective-permute-start | bytes 6291464 | tf_op jit(solution)/shard_map/ppermute | solution.py:14
  9.3 119.9 %collective-permute-start = (bf16[256,6,1024]{2,0,1:T(8,128)(2,1)}, bf16[256,6,1024]{2,0,1:T(8,128)(2,1)}, u32[]{:S(2)}, u32[]{:S(2)}) collective-permute-start(bf16[256,6,1024]{2,0,1:T(8,128)(2,1)} %bitcast.187), channel_id=1, source_target_pairs={{28,0},{0,4},{4,8},{8,12},{12,16},{16,20},{20,24},{24,28},{29,1},{... | collective-permute-start | bytes 9437192 | tf_op jit(solution)/shard_map/ppermute | solution.py:14
  129.1 21.9 %copy-start.5 = (bf16[1,6,6,4,4]{2,4,3,1,0:T(4,128)(2,1)S(1)}, bf16[1,6,6,4,4]{2,4,3,1,0:T(4,128)(2,1)}, u32[]{:S(2)}) copy-start(bf16[1,6,6,4,4]{2,4,3,1,0:T(4,128)(2,1)} %param.11) | copy-start | bytes 3460
  271.7 1.9 copy-start.4
  466.7 1.9 copy-start.3
  779.7 4.3 copy-start.2
  805.1 10.8 %copy-start.1 = (bf16[1,1024,4,256]{3,2,1,0:T(4,128)(2,1)S(1)}, bf16[1,1024,4,256]{3,2,1,0:T(4,128)(2,1)}, u32[]{:S(2)}) copy-start(bf16[1,1024,4,256]{3,2,1,0:T(4,128)(2,1)} %param.10) | copy-start | bytes 6291460
Sparse Core Ops, SparseCore 0:
  9.8 105.0 all-gather.6
  116.8 122.3 all-gather.8
  288.9 157.2 all-gather.10
